TPU v7x, 128 devices: a whole 4x4x4 slice. The times are simulated.
128 devices in a mesh: dp: 16 (over y, z), mp: 8 (over x, core).
Axes of the slice: x: 4, y: 4, z: 4, core: 2. Of those that a mesh axis runs over, the one named last changes fastest.
Arguments:
- grad_out: bfloat16 [16384, 6144], P(('dp', 'mp')), may hold values from -40 to 40
- context: bfloat16 [16384, 6144], P('dp', 'mp'), may hold values from -47 to 47
- weight: bfloat16 [6144, 6144], P(None, 'mp'), may hold values from -0.078125 to 0.078125
- master: float32 [6144, 6144], P('dp', 'mp'), may hold values from -0.6 to 0.6
- moment_q: bfloat16 [6144, 6144], P('dp', 'mp'), may hold values from -440 to 440
- second_moment: float32 [6144, 6144], P('dp', 'mp'), may hold values from 0.02 to 1
- moment_scale: float32 [], replicated, may hold values from 300 to 900
- scale_boost: float32 [], replicated, may hold values from 1.25 to 2
Outputs:
- input_grad: bfloat16 [16384, 6144], P('dp', 'mp')
- new_master: float32 [6144, 6144], P('dp', 'mp')
- new_moment_q: bfloat16 [6144, 6144], P('dp', 'mp')
- new_second: float32 [6144, 6144], P('dp', 'mp')
- new_scale: float32 [], replicated
- grad_scale: float32 [], replicated
- new_weight: bfloat16 [6144, 6144], P(None, 'mp')
All inputs are finite; a program needn't handle non-finite values. Where the computation divides by a largest or mean magnitude, that divisor is 1e-20 or more.
Results may differ from a plain program's by a relative error of at most 0.014.
Values may be sent and summed in bfloat16 or wider, within the bound.
No kernel may reach another device: no remote copies, remote signals or barrier semaphores. Data moves between devices by JAX's collectives and lax.ppermute only.
A program may use at most 128 MiB of HBM per device.

v0:
```python
import math
import jax
import jax.numpy as jnp
from jax import lax
from jax.sharding import PartitionSpec as P

D = 6144
HD = 6144
N_DEV = 128
LANES = 128
quant_top = 448.0
peak_eps = 1e-06
norm_eps = 1e-06
clip_rms = 0.5
beta_one = 0.9
beta_two = 0.95
bias_one = 1.0 - 0.9**10
bias_two = 1.0 - 0.95**10
adam_eps = 1e-08
rate_value = 0.01
decay_value = 0.1
contract_rows = (((0,), (0,)), ((), ()))


def input_product(full_grad, weight):
    return jnp.dot(full_grad, weight, preferred_element_type=jnp.float32).astype(jnp.bfloat16)


def spread(value):
    rows = jnp.broadcast_to(value, (N_DEV, LANES))
    return lax.all_to_all(rows, ("dp", "mp"), 0, 0, tiled=True)


def global_max(value):
    return jnp.max(spread(value))


def global_sum(value):
    return jnp.sum(spread(value)[:, 0])


def weight_gradient(full_grad, context, scale_boost):
    held = lax.dot_general(full_grad, context, contract_rows, preferred_element_type=jnp.float32)
    local_peak = jnp.max(jnp.abs(held))
    peak = global_max(local_peak)
    grad_scale = quant_top * scale_boost / (peak + peak_eps)
    scaled = held * grad_scale
    summed = lax.psum_scatter(
        jnp.clip(scaled, -quant_top, quant_top).astype(jnp.bfloat16),
        "dp",
        scatter_dimension=0,
        tiled=True,
    ).astype(jnp.float32)
    return (summed, grad_scale)


def local(grad_out, context, weight, master, moment_q, second_moment, moment_scale, scale_boost):
    full_grad = lax.all_gather(grad_out, "mp", axis=0, tiled=True)
    input_grad = input_product(full_grad, weight)
    summed, grad_scale = weight_gradient(full_grad, context, scale_boost)
    gradient = summed / grad_scale
    squares = global_sum(jnp.sum(gradient * gradient))
    norm_value = jnp.sqrt(squares + norm_eps)
    clip_factor = clip_rms * math.sqrt(D * HD) / norm_value
    step_grad = clip_factor * gradient
    old_moment = moment_q.astype(jnp.float32) / moment_scale
    moment = beta_one * old_moment + (1.0 - beta_one) * step_grad
    new_second = beta_two * second_moment + (1.0 - beta_two) * step_grad * step_grad
    update = moment / bias_one / (jnp.sqrt(new_second / bias_two) + adam_eps) + decay_value * master
    new_master = master - rate_value * update
    moment_top = global_max(jnp.max(jnp.abs(moment)))
    new_scale = quant_top / (moment_top + peak_eps)
    new_moment_q = (moment * new_scale).astype(jnp.bfloat16)
    new_weight = lax.all_gather(new_master.astype(jnp.bfloat16), "dp", axis=0, tiled=True)
    return (input_grad, new_master, new_moment_q, new_second, new_scale, grad_scale, new_weight)


def solution(mesh):
    return jax.shard_map(
        local,
        mesh=mesh,
        in_specs=(
            P(("dp", "mp"), None),
            P("dp", "mp"),
            P(None, "mp"),
            P("dp", "mp"),
            P("dp", "mp"),
            P("dp", "mp"),
            P(),
            P(),
        ),
        out_specs=(
            P("dp", "mp"),
            P("dp", "mp"),
            P("dp", "mp"),
            P("dp", "mp"),
            P(),
            P(),
            P(None, "mp"),
        ),
        check_vma=False,
    )
```

profile of v0, /device:TPU:1, one launch (start us, length us, event | category | flops | bytes accessed | tf_op | source)
XLA Modules:
  0.0 329.5 jit_solution(7558855803893621168)
XLA Ops:
  7.2 0.0 copy-start
  7.2 0.0 all-gather.3.cloned.1.call-start
  7.2 0.7 all-gather.3.cloned.1.call-update
  7.9 72.8 %all-gather.3.cloned.1.call-done = bf16[1024,6144]{1,0:T(8,128)(2,1)} async-done(((bf16[128,6144]{1,0:T(8,128)(2,1)}), bf16[1024,6144]{1,0:T(8,128)(2,1)}) %all-gather.3.cloned.1.call-update) | async-done | bytes 12582928 | tf_op jit(solution)/shard_map/all_gather | solution.py:58
  80.7 0.0 copy-done
  80.7 17.7 %abs_reduce_fusion = (f32[]{:T(128)}, f32[6144,768]{1,0:T(8,128)}) fusion(bf16[1024,6144]{1,0:T(8,128)(2,1)} %all-gather.3.cloned.1.call-done, bf16[1024,768]{1,0:T(8,128)(2,1)S(1)} %copy-done), kind=kOutput, calls=%fused_computation.1 | convolution fusion | flops 9673113600 | bytes 33030148 | tf_op jit(solution)/shard_map/dot_general | solution.py:43
  98.3 1.3 broadcast_in_dim.9
  99.6 8.3 %all-to-all-start = ((f32[128,1,128]{2,1,0:T(1,128)}), f32[128,1,128]{2,1,0:T(1,128)S(1)}, u32[]{:S(2)}, u32[]{:S(2)}) async-start(f32[128,1,128]{2,1,0:T(1,128)} %broadcast_in_dim.9), calls=%async_computation | async-start | bytes 131072 | tf_op jit(solution)/shard_map/all_to_all | solution.py:31
  107.9 0.0 reduce-scatter.2.cloned.1.call-start
  108.6 8.7 %all-to-all-done = f32[128,1,128]{2,1,0:T(1,128)S(1)} async-done(((f32[128,1,128]{2,1,0:T(1,128)}), f32[128,1,128]{2,1,0:T(1,128)S(1)}, u32[]{:S(2)}, u32[]{:S(2)}) %all-to-all-start) | async-done | bytes 65568 | tf_op jit(solution)/shard_map/all_to_all | solution.py:31
  117.3 0.6 reduce_max.37
  118.6 11.6 %clamp_convert_fusion = bf16[6144,768]{1,0:T(8,128)(2,1)} fusion(f32[6144,768]{1,0:T(8,128)} %get-tuple-element.12, f32[]{:T(128)} %div.38), kind=kLoop, calls=%fused_computation | loop fusion | flops 14155776 | bytes 28311556 | tf_op jit(solution)/shard_map/convert_element_type | solution.py:49
  130.2 0.0 copy-start.3
  130.2 0.0 reduce-scatter.2.cloned.1.call-update
  130.2 83.3 %reduce-scatter.2.cloned.1.call-done = bf16[384,768]{1,0:T(8,128)(2,1)} async-done(((bf16[6144,768]{1,0:T(8,128)(2,1)}), bf16[384,768]{1,0:T(8,128)(2,1)}) %reduce-scatter.2.cloned.1.call-update) | async-done | bytes 589840 | tf_op jit(solution)/shard_map/reduce_scatter | solution.py:48
  213.5 0.0 copy-start.2
  213.5 2.0 multiply_reduce_fusion
  215.5 1.3 broadcast_in_dim.10
  216.8 8.3 %all-to-all-start.1 = ((f32[128,1,128]{2,1,0:T(1,128)}), f32[128,1,128]{2,1,0:T(1,128)S(1)}, u32[]{:S(2)}, u32[]{:S(2)}) async-start(f32[128,1,128]{2,1,0:T(1,128)} %broadcast_in_dim.10), calls=%async_computation.2 | async-start | bytes 131072 | tf_op jit(solution)/shard_map/all_to_all | solution.py:31
  225.1 0.0 all-gather.5.cloned.1.call-start
  225.8 8.7 %all-to-all-done.1 = f32[128,1,128]{2,1,0:T(1,128)S(1)} async-done(((f32[128,1,128]{2,1,0:T(1,128)}), f32[128,1,128]{2,1,0:T(1,128)S(1)}, u32[]{:S(2)}, u32[]{:S(2)}) %all-to-all-start.1) | async-done | bytes 65568 | tf_op jit(solution)/shard_map/all_to_all | solution.py:31
  234.5 0.6 slice_reduce_fusion
  235.9 0.0 copy-done.3
  235.9 0.0 copy-done.2
  235.9 4.1 %fusion.1 = (bf16[384,768]{1,0:T(8,128)(2,1)}, f32[384,768]{1,0:T(8,128)}, f32[384,768]{1,0:T(8,128)S(1)}, f32[384,768]{1,0:T(8,128)}) fusion(f32[384,768]{1,0:T(8,128)S(1)} %copy-done.3, f32[]{:T(128)} %div.38, bf16[384,768]{1,0:T(8,128)(2,1)S(1)} %copy-done.2, f32[]{:T(128)S(6)} %div.41, f32[]{:T(128)S(6)} %copy.20, bf16[384,768]{1,0:T(8,128)(2,1)} %param.12, ...), kind=kLoop, calls=%fused_computation.12 | loop fusion | flops 6193152 | bytes 7667724 | tf_op jit(solution)/shard_map/convert_element_type | solution.py:74
  240.0 0.0 all-gather.5.cloned.1.call-update
  240.0 0.7 abs_reduce_fusion.1
  240.7 1.3 broadcast_in_dim.11
  242.0 4.6 %all-to-all-start.2 = ((f32[128,1,128]{2,1,0:T(1,128)}), f32[128,1,128]{2,1,0:T(1,128)S(1)}, u32[]{:S(2)}, u32[]{:S(2)}) async-start(f32[128,1,128]{2,1,0:T(1,128)} %broadcast_in_dim.11), calls=%async_computation.3 | async-start | bytes 131072 | tf_op jit(solution)/shard_map/all_to_all | solution.py:31
  246.6 15.8 %convolution_convert_fusion = bf16[1024,768]{1,0:T(8,128)(2,1)} fusion(bf16[1024,6144]{1,0:T(8,128)(2,1)} %all-gather.3.cloned.1.call-done, bf16[6144,768]{1,0:T(8,128)(2,1)} %param.10), kind=kOutput, calls=%fused_computation.3 | convolution fusion | flops 9664462848 | bytes 23592960 | tf_op jit(solution)/shard_map/dot_general | solution.py:26
  262.5 0.0 all-to-all-done.2
  262.5 0.6 reduce_max.39
  263.8 0.9 multiply_convert_fusion
  264.7 48.0 %all-gather.5.cloned.1.call-done = bf16[6144,768]{1,0:T(8,128)(2,1)} async-done(((bf16[384,768]{1,0:T(8,128)(2,1)}), bf16[6144,768]{1,0:T(8,128)(2,1)}) %all-gather.5.cloned.1.call-update) | async-done | bytes 9437200 | tf_op jit(solution)/shard_map/all_gather | solution.py:74
  312.6 0.0 copy-start.1
  312.6 8.1 %copy.22 = bf16[6144,768]{1,0:T(8,128)(2,1)} copy(bf16[6144,768]{1,0:T(8,128)(2,1)} %all-gather.5.cloned.1.call-done) | data formatting | bytes 18874368
  320.8 0.0 copy-done.1
Async XLA Ops:
  7.2 73.5 %copy-start = (bf16[1024,768]{1,0:T(8,128)(2,1)S(1)}, bf16[1024,768]{1,0:T(8,128)(2,1)}, u32[]{:S(2)}) copy-start(bf16[1024,768]{1,0:T(8,128)(2,1)} %param.9) | copy-start | bytes 4718596
  7.2 73.5 %all-gather.3.cloned.1.call-start = ((), (), s32[]{:S(2)}) async-start(), calls=%async_computation.4 | async-start | bytes 14155776 | tf_op jit(solution)/shard_map/all_gather | solution.py:58
  99.6 17.7 %all-to-all-start = ((f32[128,1,128]{2,1,0:T(1,128)}), f32[128,1,128]{2,1,0:T(1,128)S(1)}, u32[]{:S(2)}, u32[]{:S(2)}) async-start(f32[128,1,128]{2,1,0:T(1,128)} %broadcast_in_dim.9), calls=%async_computation | async-start | bytes 131072 | tf_op jit(solution)/shard_map/all_to_all | solution.py:31
  107.9 105.6 %reduce-scatter.2.cloned.1.call-start = ((), (), s32[]{:S(2)}) async-start(), calls=%async_computation.5 | async-start | bytes 10027008 | tf_op jit(solution)/shard_map/reduce_scatter | solution.py:48
  130.2 105.7 %copy-start.3 = (f32[384,768]{1,0:T(8,128)S(1)}, f32[384,768]{1,0:T(8,128)}, u32[]{:S(2)}) copy-start(f32[384,768]{1,0:T(8,128)} %param.11) | copy-start | bytes 3538948
  213.5 22.4 %copy-start.2 = (bf16[384,768]{1,0:T(8,128)(2,1)S(1)}, bf16[384,768]{1,0:T(8,128)(2,1)}, u32[]{:S(2)}) copy-start(bf16[384,768]{1,0:T(8,128)(2,1)} %reduce-scatter.2.cloned.1.call-done) | copy-start | bytes 1769476
  216.8 17.7 %all-to-all-start.1 = ((f32[128,1,128]{2,1,0:T(1,128)}), f32[128,1,128]{2,1,0:T(1,128)S(1)}, u32[]{:S(2)}, u32[]{:S(2)}) async-start(f32[128,1,128]{2,1,0:T(1,128)} %broadcast_in_dim.10), calls=%async_computation.2 | async-start | bytes 131072 | tf_op jit(solution)/shard_map/all_to_all | solution.py:31
  225.1 87.5 %all-gather.5.cloned.1.call-start = ((), (), s32[]{:S(2)}) async-start(), calls=%async_computation.6 | async-start | bytes 10027008 | tf_op jit(solution)/shard_map/all_gather | solution.py:74
  242.0 20.4 %all-to-all-start.2 = ((f32[128,1,128]{2,1,0:T(1,128)}), f32[128,1,128]{2,1,0:T(1,128)S(1)}, u32[]{:S(2)}, u32[]{:S(2)}) async-start(f32[128,1,128]{2,1,0:T(1,128)} %broadcast_in_dim.11), calls=%async_computation.3 | async-start | bytes 131072 | tf_op jit(solution)/shard_map/all_to_all | solution.py:31
  312.6 8.2 %copy-start.1 = (bf16[1024,768]{1,0:T(8,128)(2,1)S(1)}, bf16[1024,768]{1,0:T(8,128)(2,1)}, u32[]{:S(2)}) copy-start(bf16[1024,768]{1,0:T(8,128)(2,1)} %param.9) | copy-start | bytes 4718596
Sparse Core Ops, SparseCore 0:
  9.7 70.9 all-gather.2
  130.3 83.0 reduce-scatter.1
  240.1 72.4 all-gather.4
where the time goes:
time: 330 us
  waiting for transfers between devices  222 us (67%)
  matrix products  33.5 us (10%)
  starting transfers between devices  21.3 us (6%)
  other arithmetic  21.1 us (6%)
  between operations  19.4 us (6%)
  local copies, waits for them, and re-layouts  12.1 us (4%)
    reduce_scatter x1, waiting for transfers between devices, weight_gradient(): lax.psum_scatter(jnp.clip(scaled, -quant_top, quant_top).astype(jnp.bfloa...  83.3 us
    all_gather x1, waiting for transfers between devices, local(): full_grad = lax.all_gather(grad_out, 'mp', axis=0, tiled=True)  72.8 us
    all_gather x1, waiting for transfers between devices, local(): lax.all_gather(new_master.astype(jnp.bfloat16), 'dp', axis=0, tiled=True)  48 us
    all_to_all x3, starting transfers between devices, spread(): return lax.all_to_all(rows, ('dp', 'mp'), 0, 0, tiled=True)  21.1 us
    dot_general x1, matrix products, weight_gradient(): lax.dot_general(full_grad, context, contract_rows, preferred_element_type...  17.7 us
    all_to_all x3, waiting for transfers between devices, spread(): return lax.all_to_all(rows, ('dp', 'mp'), 0, 0, tiled=True)  17.5 us
    dot_general x1, matrix products, input_product(): jnp.dot(full_grad, weight, preferred_element_type=jnp.float32)  15.8 us
    convert_element_type x1, other arithmetic, weight_gradient(): jnp.clip(scaled, -quant_top, quant_top).astype(jnp.bfloat16)  11.6 us
  transfers between devices with their start and end apart: 6, of which 5 were waited for; matrix products, arithmetic and copies ran while one was open for 6% of the time, Pallas kernels for 0%

commit v1 on v0

--- a/solution.py
+++ b/solution.py
@@ -71,7 +71,12 @@
     moment_top = global_max(jnp.max(jnp.abs(moment)))
     new_scale = quant_top / (moment_top + peak_eps)
     new_moment_q = (moment * new_scale).astype(jnp.bfloat16)
-    new_weight = lax.all_gather(new_master.astype(jnp.bfloat16), "dp", axis=0, tiled=True)
+    new_weight = jnp.concatenate(
+        lax.all_to_all(
+            jnp.stack([new_master.astype(jnp.bfloat16)] * lax.axis_size("dp")), "dp", 0, 0
+        ),
+        axis=0,
+    )
     return (input_grad, new_master, new_moment_q, new_second, new_scale, grad_scale, new_weight)
 
 

time: 330 us -> 451 us (1.37); the launches traced: 330 us -> 442 us
  waiting for transfers between devices: 222 us -> 317 us
  blocking collectives: 0 us -> 13.9 us
    all_to_all x0 -> x1, waiting for transfers between devices: none -> 143 us  [local(): lax.all_to_all(jnp.stack([new_master.astype(jnp.bfloat16)] * lax.axis_siz...]
    all_gather x1 -> x0, waiting for transfers between devices: 48 us -> none  [local(): lax.all_gather(new_master.astype(jnp.bfloat16), 'dp', axis=0, tiled=True)]
    all_to_all x0 -> x1, blocking collectives: none -> 13.9 us  [spread(): return lax.all_to_all(rows, ('dp', 'mp'), 0, 0, tiled=True)]
    all_to_all x0 -> x1, starting transfers between devices: none -> 4.96 us  [local(): lax.all_to_all(jnp.stack([new_master.astype(jnp.bfloat16)] * lax.axis_siz...]
    another operation x0 -> x1, local copies, waits for them, and re-layouts: none -> 4.66 us  [local(): jnp.stack([new_master.astype(jnp.bfloat16)] * lax.axis_size('dp'))]
    all_to_all x3 -> x2, starting transfers between devices: 21.1 us -> 16.5 us  [spread(): return lax.all_to_all(rows, ('dp', 'mp'), 0, 0, tiled=True)]
    all_to_all x3 -> x2, waiting for transfers between devices: 17.5 us -> 17.5 us  [spread(): return lax.all_to_all(rows, ('dp', 'mp'), 0, 0, tiled=True)]
  transfers between devices with their start and end apart: 6 -> 5, of which waited for: 5 -> 5; matrix products, arithmetic and copies ran while one was open for 6% -> 4% of each run, Pallas kernels for 0% -> 0%
where the time goes in v1:
time: 451 us; the launch traced here: 442 us
  waiting for transfers between devices  317 us (70%)
  matrix products  33.3 us (7%)
  starting transfers between devices  21.6 us (5%)
  other arithmetic  20.9 us (5%)
  between operations  19.7 us (4%)
  local copies, waits for them, and re-layouts  16.1 us (4%)
  blocking collectives  13.9 us (3%)
    all_to_all x1, waiting for transfers between devices, local(): lax.all_to_all(jnp.stack([new_master.astype(jnp.bfloat16)] * lax.axis_siz...  143 us
    reduce_scatter x1, waiting for transfers between devices, weight_gradient(): lax.psum_scatter(jnp.clip(scaled, -quant_top, quant_top).astype(jnp.bfloa...  83.3 us
    all_gather x1, waiting for transfers between devices, local(): full_grad = lax.all_gather(grad_out, 'mp', axis=0, tiled=True)  72.8 us
    dot_general x1, matrix products, weight_gradient(): lax.dot_general(full_grad, context, contract_rows, preferred_element_type...  17.7 us
    all_to_all x2, waiting for transfers between devices, spread(): return lax.all_to_all(rows, ('dp', 'mp'), 0, 0, tiled=True)  17.5 us
    all_to_all x2, starting transfers between devices, spread(): return lax.all_to_all(rows, ('dp', 'mp'), 0, 0, tiled=True)  16.5 us
    dot_general x1, matrix products, input_product(): jnp.dot(full_grad, weight, preferred_element_type=jnp.float32)  15.6 us
    all_to_all x1, blocking collectives, spread(): return lax.all_to_all(rows, ('dp', 'mp'), 0, 0, tiled=True)  13.9 us
  transfers between devices with their start and end apart: 5, of which 5 were waited for; matrix products, arithmetic and copies ran while one was open for 4% of the time, Pallas kernels for 0%

profile of v1, /device:TPU:1, one launch (start us, length us, event | category | flops | bytes accessed | tf_op | source)
XLA Modules:
  0.0 442.4 jit_solution(1396687038744124058)
XLA Ops:
  7.2 0.0 copy-start
  7.2 0.0 all-gather.2.cloned.1.call-start
  7.2 0.7 all-gather.2.cloned.1.call-update
  7.9 72.8 %all-gather.2.cloned.1.call-done = bf16[1024,6144]{1,0:T(8,128)(2,1)} async-done(((bf16[128,6144]{1,0:T(8,128)(2,1)}), bf16[1024,6144]{1,0:T(8,128)(2,1)}) %all-gather.2.cloned.1.call-update) | async-done | bytes 12582928 | tf_op jit(solution)/shard_map/all_gather | solution.py:58
  80.7 0.0 copy-done
  80.7 17.7 %abs_reduce_fusion = (f32[]{:T(128)}, f32[6144,768]{1,0:T(8,128)}) fusion(bf16[1024,6144]{1,0:T(8,128)(2,1)} %all-gather.2.cloned.1.call-done, bf16[1024,768]{1,0:T(8,128)(2,1)S(1)} %copy-done), kind=kOutput, calls=%fused_computation.1 | convolution fusion | flops 9673113600 | bytes 33030148 | tf_op jit(solution)/shard_map/dot_general | solution.py:43
  98.3 1.3 broadcast_in_dim.9
  99.6 8.3 %all-to-all-start = ((f32[128,1,128]{2,1,0:T(1,128)}), f32[128,1,128]{2,1,0:T(1,128)S(1)}, u32[]{:S(2)}, u32[]{:S(2)}) async-start(f32[128,1,128]{2,1,0:T(1,128)} %broadcast_in_dim.9), calls=%async_computation | async-start | bytes 131072 | tf_op jit(solution)/shard_map/all_to_all | solution.py:31
  107.9 0.0 reduce-scatter.2.cloned.1.call-start
  108.6 8.7 %all-to-all-done = f32[128,1,128]{2,1,0:T(1,128)S(1)} async-done(((f32[128,1,128]{2,1,0:T(1,128)}), f32[128,1,128]{2,1,0:T(1,128)S(1)}, u32[]{:S(2)}, u32[]{:S(2)}) %all-to-all-start) | async-done | bytes 65568 | tf_op jit(solution)/shard_map/all_to_all | solution.py:31
  117.3 0.6 reduce_max.37
  118.6 11.6 %clamp_convert_fusion = bf16[6144,768]{1,0:T(8,128)(2,1)} fusion(f32[6144,768]{1,0:T(8,128)} %get-tuple-element.12, f32[]{:T(128)} %div.38), kind=kLoop, calls=%fused_computation | loop fusion | flops 14155776 | bytes 28311556 | tf_op jit(solution)/shard_map/convert_element_type | solution.py:49
  130.2 0.0 copy-start.3
  130.2 0.0 reduce-scatter.2.cloned.1.call-update
  130.2 83.3 %reduce-scatter.2.cloned.1.call-done = bf16[384,768]{1,0:T(8,128)(2,1)} async-done(((bf16[6144,768]{1,0:T(8,128)(2,1)}), bf16[384,768]{1,0:T(8,128)(2,1)}) %reduce-scatter.2.cloned.1.call-update) | async-done | bytes 589840 | tf_op jit(solution)/shard_map/reduce_scatter | solution.py:48
  213.5 0.0 copy-start.2
  213.5 2.0 multiply_reduce_fusion
  215.5 1.3 broadcast_in_dim.10
  216.8 8.3 %all-to-all-start.1 = ((f32[128,1,128]{2,1,0:T(1,128)}), f32[128,1,128]{2,1,0:T(1,128)S(1)}, u32[]{:S(2)}, u32[]{:S(2)}) async-start(f32[128,1,128]{2,1,0:T(1,128)} %broadcast_in_dim.10), calls=%async_computation.2 | async-start | bytes 131072 | tf_op jit(solution)/shard_map/all_to_all | solution.py:31
  225.8 8.8 %all-to-all-done.1 = f32[128,1,128]{2,1,0:T(1,128)S(1)} async-done(((f32[128,1,128]{2,1,0:T(1,128)}), f32[128,1,128]{2,1,0:T(1,128)S(1)}, u32[]{:S(2)}, u32[]{:S(2)}) %all-to-all-start.1) | async-done | bytes 65568 | tf_op jit(solution)/shard_map/all_to_all | solution.py:31
  234.5 0.6 slice_reduce_fusion
  235.9 0.0 copy-done.3
  235.9 0.0 copy-done.2
  235.9 3.9 fusion.1
  239.8 0.7 abs_reduce_fusion.1
  240.5 0.7 broadcast_in_dim.11
  241.2 13.9 %all_to_all.26 = f32[128,1,128]{2,1,0:T(1,128)S(1)} all-to-all(f32[128,1,128]{2,1,0:T(1,128)S(1)} %broadcast_in_dim.11), channel_id=1, replica_groups=mesh['dp'=16,'mp'=8] {'dp','mp'}, dimensions={0} | all-to-all | bytes 131072 | tf_op jit(solution)/shard_map/all_to_all | solution.py:31
  255.1 4.7 %stack.2 = bf16[16,384,768]{2,1,0:T(8,128)(2,1)} broadcast(bf16[384,768]{1,0:T(8,128)(2,1)S(1)} %get-tuple-element.7), dimensions={1,2} | broadcast | bytes 10027008 | tf_op jit(solution)/shard_map/stack | solution.py:76
  259.7 5.0 %all-to-all-start.3 = ((bf16[16,384,768]{2,1,0:T(8,128)(2,1)}), bf16[16,384,768]{2,1,0:T(8,128)(2,1)}, u32[]{:S(2)}, u32[]{:S(2)}) async-start(bf16[16,384,768]{2,1,0:T(8,128)(2,1)} %stack.2), calls=%async_computation.4 | async-start | bytes 18874368 | tf_op jit(solution)/shard_map/all_to_all | solution.py:75
  264.7 15.6 %convolution_convert_fusion = bf16[1024,768]{1,0:T(8,128)(2,1)} fusion(bf16[1024,6144]{1,0:T(8,128)(2,1)} %all-gather.2.cloned.1.call-done, bf16[6144,768]{1,0:T(8,128)(2,1)} %param.10), kind=kOutput, calls=%fused_computation.3 | convolution fusion | flops 9664462848 | bytes 23592960 | tf_op jit(solution)/shard_map/dot_general | solution.py:26
  280.4 0.6 reduce_max.39
  281.7 0.9 multiply_convert_fusion
  282.6 142.6 %all-to-all-done.3 = bf16[16,384,768]{2,1,0:T(8,128)(2,1)} async-done(((bf16[16,384,768]{2,1,0:T(8,128)(2,1)}), bf16[16,384,768]{2,1,0:T(8,128)(2,1)}, u32[]{:S(2)}, u32[]{:S(2)}) %all-to-all-start.3) | async-done | bytes 9437216 | tf_op jit(solution)/shard_map/all_to_all | solution.py:75
  425.2 0.0 copy-start.1
  425.2 8.1 %copy.22 = bf16[6144,768]{1,0:T(8,128)(2,1)} copy(bf16[6144,768]{1,0:T(8,128)(2,1)} %bitcast.3) | data formatting | bytes 18874368
  433.3 0.0 copy-done.1
Async XLA Ops:
  7.2 73.5 %copy-start = (bf16[1024,768]{1,0:T(8,128)(2,1)S(1)}, bf16[1024,768]{1,0:T(8,128)(2,1)}, u32[]{:S(2)}) copy-start(bf16[1024,768]{1,0:T(8,128)(2,1)} %param.9) | copy-start | bytes 4718596
  7.2 73.5 %all-gather.2.cloned.1.call-start = ((), (), s32[]{:S(2)}) async-start(), calls=%async_computation.5 | async-start | bytes 14155776 | tf_op jit(solution)/shard_map/all_gather | solution.py:58
  99.6 17.7 %all-to-all-start = ((f32[128,1,128]{2,1,0:T(1,128)}), f32[128,1,128]{2,1,0:T(1,128)S(1)}, u32[]{:S(2)}, u32[]{:S(2)}) async-start(f32[128,1,128]{2,1,0:T(1,128)} %broadcast_in_dim.9), calls=%async_computation | async-start | bytes 131072 | tf_op jit(solution)/shard_map/all_to_all | solution.py:31
  107.9 105.6 %reduce-scatter.2.cloned.1.call-start = ((), (), s32[]{:S(2)}) async-start(), calls=%async_computation.6 | async-start | bytes 10027008 | tf_op jit(solution)/shard_map/reduce_scatter | solution.py:48
  130.2 105.7 %copy-start.3 = (f32[384,768]{1,0:T(8,128)S(1)}, f32[384,768]{1,0:T(8,128)}, u32[]{:S(2)}) copy-start(f32[384,768]{1,0:T(8,128)} %param.11) | copy-start | bytes 3538948
  213.5 22.4 %copy-start.2 = (bf16[384,768]{1,0:T(8,128)(2,1)S(1)}, bf16[384,768]{1,0:T(8,128)(2,1)}, u32[]{:S(2)}) copy-start(bf16[384,768]{1,0:T(8,128)(2,1)} %reduce-scatter.2.cloned.1.call-done) | copy-start | bytes 1769476
  216.8 17.7 %all-to-all-start.1 = ((f32[128,1,128]{2,1,0:T(1,128)}), f32[128,1,128]{2,1,0:T(1,128)S(1)}, u32[]{:S(2)}, u32[]{:S(2)}) async-start(f32[128,1,128]{2,1,0:T(1,128)} %broadcast_in_dim.10), calls=%async_computation.2 | async-start | bytes 131072 | tf_op jit(solution)/shard_map/all_to_all | solution.py:31
  259.7 165.4 %all-to-all-start.3 = ((bf16[16,384,768]{2,1,0:T(8,128)(2,1)}), bf16[16,384,768]{2,1,0:T(8,128)(2,1)}, u32[]{:S(2)}, u32[]{:S(2)}) async-start(bf16[16,384,768]{2,1,0:T(8,128)(2,1)} %stack.2), calls=%async_computation.4 | async-start | bytes 18874368 | tf_op jit(solution)/shard_map/all_to_all | solution.py:75
  425.2 8.2 %copy-start.1 = (bf16[1024,768]{1,0:T(8,128)(2,1)S(1)}, bf16[1024,768]{1,0:T(8,128)(2,1)}, u32[]{:S(2)}) copy-start(bf16[1024,768]{1,0:T(8,128)(2,1)} %param.9) | copy-start | bytes 4718596
Sparse Core Ops, SparseCore 0:
  9.7 70.9 all-gather.1
  130.3 83.0 reduce-scatter.1
